TPU v7x, 512 devices: a whole 4x4x16 slice. The times are simulated.
512 devices in a mesh: tm: 32 (over z, core), bat: 16 (over y, x).
Axes of the slice: x: 4, y: 4, z: 16, core: 2. Of those that a mesh axis runs over, the one named last changes fastest.
Arguments:
- power0: float32 [512, 6144], P('tm', 'bat'), may hold values from -0.5 to 0.5
- charge0: float32 [512, 6144], P('tm', 'bat'), may hold values from 0 to 1
- dyn_dual0: float32 [512, 6144], P('tm', 'bat'), may hold values from -3 to 3
- feeder_dual0: float32 [512, 3072], P(('tm', 'bat')), may hold values from 0 to 0.5
- price: float32 [512, 6144], P('tm', 'bat'), may hold values from -12 to 12
- inflow: float32 [512, 6144], P('tm', 'bat'), may hold values from -1.5 to 1.5
- power_limit: float32 [6144], P('bat'), may hold values from 0.5 to 6
- capacity: float32 [6144], P('bat'), may hold values from 0.5 to 8
- feeder_limit: float32 [3072], replicated, may hold values from 0 to 1
- block_values: float32 [72, 128, 128], replicated, may hold values from -0.3125 to 0.3125
- block_cols: int32 [72], replicated, may hold values from 0 to 47, as said below
- block_offsets: int32 [25], replicated, may hold values from 0 to 72, as said below
Outputs:
- power: float32 [512, 6144], P('tm', 'bat')
- charge: float32 [512, 6144], P('tm', 'bat')
- dyn_dual: float32 [512, 6144], P('tm', 'bat')
- feeder_dual: float32 [512, 3072], P(('tm', 'bat'))
Inputs may be any that keep to these rules, and one draw needn't show every extreme that they name: `block_cols`: every battery block 0 to 47 appears at least once. block_offsets[0] = 0, strictly rising, block_offsets[24] = 72.
All inputs are finite; a program needn't handle non-finite values.
Results may differ from a plain program's by a relative error of at most 0.0001.
Values sent between devices are 32-bit elements; how exact they have to be, the bound alone decides.
No kernel may reach another device: no remote copies, remote signals or barrier semaphores. Data moves between devices by JAX's collectives and lax.ppermute only.
A program may use at most 64 MiB of HBM per device.

v0:
```python
import jax
import jax.numpy as jnp
from jax import lax
from jax.sharding import PartitionSpec as P

ITERS = 4
HIGH = lax.Precision.HIGHEST
ETA_STEP = 0.4
EPS_NORM = 1e-06


def shifted(block, axis, distance):
    devices = range(lax.axis_size(axis))
    route = [(i - distance, i) for i in devices if i - distance in devices]
    return lax.ppermute(block, axis, route)


def row_table(block_offsets, count):
    index_all = jnp.arange(count, dtype=jnp.int32)
    row_of = jnp.sum((index_all[:, None] >= block_offsets[None, 1:-1]).astype(jnp.int32), axis=1)
    feed_count = block_offsets.shape[0] - 1
    return (row_of[:, None] == jnp.arange(feed_count, dtype=jnp.int32)[None, :]).astype(jnp.float32)


def feeder_apply(field, block_values, rows_tab, cols_tab):
    count_rows = field.shape[0]
    blk = block_values.shape[1]
    blocks = field.reshape(count_rows, -1, blk)
    picked = jnp.einsum("rnk,jn->rjk", blocks, cols_tab, precision=HIGH)
    partial_rows = jnp.einsum("rjk,jmk->rjm", picked, block_values, precision=HIGH)
    summed = jnp.einsum("rjm,jf->rfm", partial_rows, rows_tab, precision=HIGH)
    return summed.reshape(count_rows, -1)


def feeder_adjoint(duals, block_values, rows_tab, cols_tab):
    count_rows = duals.shape[0]
    blk = block_values.shape[1]
    blocks = duals.reshape(count_rows, -1, blk)
    chosen = jnp.einsum("rfm,jf->rjm", blocks, rows_tab, precision=HIGH)
    pushed = jnp.einsum("rjm,jmk->rjk", chosen, block_values, precision=HIGH)
    spread = jnp.einsum("rjk,jn->rnk", pushed, cols_tab, precision=HIGH)
    return spread.reshape(count_rows, -1)


def shards(
    power0,
    charge0,
    dyn_dual0,
    feeder_dual0,
    price,
    inflow,
    power_limit,
    capacity,
    feeder_limit,
    block_values,
    block_cols,
    block_offsets,
):
    blk = block_values.shape[1]
    rows_tab = row_table(block_offsets, block_values.shape[0])
    local_batteries = power0.shape[1]
    local_blocks = local_batteries // blk
    first_block = lax.axis_index("bat") * local_blocks
    inside = (block_cols >= first_block) & (block_cols < first_block + local_blocks)
    local_cols = jnp.clip(block_cols - first_block, 0, local_blocks - 1)
    local_tab = (
        (local_cols[:, None] == jnp.arange(local_blocks, dtype=jnp.int32)[None, :])
        & inside[:, None]
    ).astype(jnp.float32)

    def couple_backward(duals):
        return feeder_adjoint(
            lax.all_gather(duals, "bat", axis=0, tiled=True), block_values, rows_tab, local_tab
        )

    power, charge, dyn_dual, feeder_dual = (power0, charge0, dyn_dual0, feeder_dual0)
    weight = jnp.asarray(1.0, dtype=jnp.float32)
    pushed = couple_backward(feeder_dual)
    limit_row = power_limit[None, :]
    for iteration in range(ITERS):
        step_primal = ETA_STEP / weight
        step_dual = ETA_STEP * weight
        following = shifted(dyn_dual[:1], "tm", -1)
        dual_next = jnp.concatenate([dyn_dual[1:], following], axis=0)
        power_new = jnp.clip(
            power - step_primal * (price - dyn_dual + pushed), -limit_row, limit_row
        )
        charge_new = jnp.clip(charge - step_primal * (dyn_dual - dual_next), 0.0, capacity[None, :])
        power_bar = 2.0 * power_new - power
        charge_bar = 2.0 * charge_new - charge
        last_iteration = iteration + 1 == ITERS
        if not last_iteration:
            move_power = power_new - power
            move_charge = charge_new - charge
            primal_local = jnp.sum(move_power * move_power + move_charge * move_charge)
            primal_sq = lax.psum(primal_local, ("tm", "bat"))
        coupled = lax.psum_scatter(
            feeder_apply(power_bar, block_values, rows_tab, local_tab),
            "bat",
            scatter_dimension=0,
            tiled=True,
        )
        preceding = shifted(charge_bar[-1:], "tm", 1)
        charge_prev = jnp.concatenate([preceding, charge_bar[:-1]], axis=0)
        dyn_new = dyn_dual + step_dual * (charge_bar - charge_prev - power_bar - inflow)
        feeder_new = jnp.maximum(0.0, feeder_dual + step_dual * (coupled - feeder_limit[None, :]))
        if not last_iteration:
            move_dyn = dyn_new - dyn_dual
            move_feed = feeder_new - feeder_dual
            dual_local = jnp.sum(move_dyn * move_dyn) + jnp.sum(move_feed * move_feed)
            dual_sq = lax.psum(dual_local, ("tm", "bat"))
            weight = jnp.sqrt(weight * jnp.sqrt((dual_sq + EPS_NORM) / (primal_sq + EPS_NORM)))
            pushed = couple_backward(feeder_new)
        power, charge, dyn_dual, feeder_dual = (power_new, charge_new, dyn_new, feeder_new)
    return (power, charge, dyn_dual, feeder_dual)


def solution(mesh):
    return jax.shard_map(
        shards,
        mesh=mesh,
        in_specs=(
            P("tm", "bat"),
            P("tm", "bat"),
            P("tm", "bat"),
            P(("tm", "bat"), None),
            P("tm", "bat"),
            P("tm", "bat"),
            P("bat"),
            P("bat"),
            P(),
            P(),
            P(),
            P(),
        ),
        out_specs=(P("tm", "bat"), P("tm", "bat"), P("tm", "bat"), P(("tm", "bat"), None)),
        check_vma=False,
    )
```

profile of v0, /device:TPU:2, one launch (start us, length us, event | category | flops | bytes accessed | tf_op | source)
XLA Modules:
  0.0 976.7 jit_solution(11067665464385182962)
XLA Ops:
  11.4 26.6 %all-gather = f32[16,1,3072]{2,1,0:T(1,128)S(1)} all-gather(f32[1,1,3072]{2,1,0:T(1,128)} %bitcast.181), channel_id=1, replica_groups=mesh['tm'=32,'bat'=16] {'bat'}, dimensions={0}, use_global_device_ids=true | all-gather | bytes 208896 | tf_op jit(solution)/shard_map/all_gather | solution.py:73
  38.5 5.8 convolution_bitcast_fusion.15
  48.7 9.2 convolution_bitcast_fusion.14
  61.8 115.7 %all-reduce.12.cloned.1.call-done = f32[16,3072]{1,0:T(8,128)} async-done(((f32[16,3072]{1,0:T(8,128)}), f32[16,3072]{1,0:T(8,128)}) %all-reduce.12.cloned.1.call-update) | async-done | bytes 196624
  177.5 2.2 multiply_reduce_fusion.5
  179.7 22.0 %all-gather.1 = f32[16,1,3072]{2,1,0:T(1,128)S(1)} all-gather(f32[1,1,3072]{2,1,0:T(1,128)S(1)} %bitcast.179), channel_id=1, replica_groups=mesh['tm'=32,'bat'=16] {'bat'}, dimensions={0}, use_global_device_ids=true | all-gather | bytes 208896 | tf_op jit(solution)/shard_map/all_gather | solution.py:73
  202.1 5.8 convolution_bitcast_fusion.13
  209.7 103.0 %all-reduce.6 = (f32[]{:T(128)}, f32[]{:T(128)}) all-reduce(f32[]{:T(128)S(6)} %add.99, f32[]{:T(128)} %get-tuple-element.31), channel_id=1, replica_groups=mesh['tm'=32,'bat'=16] {'tm','bat'}, use_global_device_ids=true, to_apply=%region_4.5 | all-reduce | flops 2 | bytes 16 | tf_op jit(solution)/shard_map/psum | solution.py:111
  314.8 1.9 collective-permute-start.3
  318.5 9.2 convolution_bitcast_fusion.12
  330.3 110.9 %all-reduce.14.cloned.1.call-done = f32[16,3072]{1,0:T(8,128)} async-done(((f32[16,3072]{1,0:T(8,128)}), f32[16,3072]{1,0:T(8,128)}) %all-reduce.14.cloned.1.call-update) | async-done | bytes 196624
  441.1 2.2 multiply_reduce_fusion.4
  443.3 22.0 %all-gather.2 = f32[16,1,3072]{2,1,0:T(1,128)S(1)} all-gather(f32[1,1,3072]{2,1,0:T(1,128)S(1)} %bitcast.178), channel_id=1, replica_groups=mesh['tm'=32,'bat'=16] {'bat'}, dimensions={0}, use_global_device_ids=true | all-gather | bytes 208896 | tf_op jit(solution)/shard_map/all_gather | solution.py:73
  465.7 5.8 convolution_bitcast_fusion.11
  473.3 103.0 %all-reduce.5 = (f32[]{:T(128)}, f32[]{:T(128)}) all-reduce(f32[]{:T(128)S(6)} %add.106, f32[]{:T(128)} %get-tuple-element.23), channel_id=1, replica_groups=mesh['tm'=32,'bat'=16] {'tm','bat'}, use_global_device_ids=true, to_apply=%region_10.11 | all-reduce | flops 2 | bytes 16 | tf_op jit(solution)/shard_map/psum | solution.py:111
  582.1 9.2 convolution_bitcast_fusion.10
  593.8 110.9 %all-reduce.16.cloned.1.call-done = f32[16,3072]{1,0:T(8,128)} async-done(((f32[16,3072]{1,0:T(8,128)}), f32[16,3072]{1,0:T(8,128)}) %all-reduce.16.cloned.1.call-update) | async-done | bytes 196624
  704.7 2.2 multiply_reduce_fusion.3
  706.9 22.2 %all-gather.3 = f32[16,1,3072]{2,1,0:T(1,128)S(1)} all-gather(f32[1,1,3072]{2,1,0:T(1,128)S(1)} %bitcast.180), channel_id=1, replica_groups=mesh['tm'=32,'bat'=16] {'bat'}, dimensions={0}, use_global_device_ids=true | all-gather | bytes 208896 | tf_op jit(solution)/shard_map/all_gather | solution.py:73
  729.5 5.8 convolution_bitcast_fusion.9
  736.7 103.0 %all-reduce.4 = (f32[]{:T(128)}, f32[]{:T(128)}) all-reduce(f32[]{:T(128)S(6)} %add.113, f32[]{:T(128)} %get-tuple-element.15), channel_id=1, replica_groups=mesh['tm'=32,'bat'=16] {'tm','bat'}, use_global_device_ids=true, to_apply=%region_16.17 | all-reduce | flops 2 | bytes 16 | tf_op jit(solution)/shard_map/psum | solution.py:111
  845.4 9.2 convolution_bitcast_fusion.8
  855.8 112.2 %all-reduce.18.cloned.1.call-done = f32[16,3072]{1,0:T(8,128)} async-done(((f32[16,3072]{1,0:T(8,128)}), f32[16,3072]{1,0:T(8,128)}) %all-reduce.18.cloned.1.call-update) | async-done | bytes 196624
  968.0 2.1 fusion.92
  (95 shorter events, 32.2 us)
Async XLA Ops:
  7.2 37.6 %copy-start.2 = (f32[16,384]{1,0:T(8,128)S(1)}, f32[16,384]{1,0:T(8,128)}, u32[]{:S(2)}) copy-start(f32[16,384]{1,0:T(8,128)} %param.14) | copy-start | bytes 73732
  7.2 37.6 %copy-start.6 = (f32[384]{0:T(512)S(1)}, f32[384]{0:T(512)}, u32[]{:S(2)}) copy-start(f32[384]{0:T(512)} %param.18) | copy-start | bytes 4612
  7.2 37.6 %copy-start.4 = (f32[16,384]{1,0:T(8,128)S(1)}, f32[16,384]{1,0:T(8,128)}, u32[]{:S(2)}) copy-start(f32[16,384]{1,0:T(8,128)} %param.12) | copy-start | bytes 73732
  7.2 37.6 %copy-start.5 = (f32[16,384]{1,0:T(8,128)S(1)}, f32[16,384]{1,0:T(8,128)}, u32[]{:S(2)}) copy-start(f32[16,384]{1,0:T(8,128)} %param.13) | copy-start | bytes 73732
  7.2 37.6 %copy-start.1 = (f32[16,384]{1,0:T(8,128)S(1)}, f32[16,384]{1,0:T(8,128)}, u32[]{:S(2)}) copy-start(f32[16,384]{1,0:T(8,128)} %param.16) | copy-start | bytes 73732
  7.2 37.6 %copy-start.8 = (f32[384]{0:T(512)S(1)}, f32[384]{0:T(512)}, u32[]{:S(2)}) copy-start(f32[384]{0:T(512)} %param.19) | copy-start | bytes 4612
  7.2 40.4 %copy-start = (f32[16,384]{1,0:T(8,128)S(1)}, f32[16,384]{1,0:T(8,128)}, u32[]{:S(2)}) copy-start(f32[16,384]{1,0:T(8,128)} %param.17) | copy-start | bytes 73732
  7.2 170.3 %all-reduce.12.cloned.1.call-start = ((), (), s32[]{:S(2)}) async-start(), calls=%async_computation | async-start | bytes 393216
  8.0 36.8 %collective-permute-start = (f32[1,384]{1,0:T(1,128)S(1)}, f32[1,384]{1,0:T(1,128)S(1)}, u32[]{:S(2)}, u32[]{:S(2)}) collective-permute-start(f32[1,384]{1,0:T(1,128)S(1)} %slice.53), channel_id=1, source_target_pairs={{16,0},{32,16},{48,32},{64,48},{80,64},{96,80},{112,96},{128,112},... | collective-permute-start | bytes 4616 | tf_op jit(solution)/shard_map/ppermute | solution.py:15
  44.3 133.2 %copy-start.3 = (f32[3072]{0:T(1024)S(1)}, f32[3072]{0:T(1024)}, u32[]{:S(2)}) copy-start(f32[3072]{0:T(1024)} %param.20) | copy-start | bytes 36868
  44.3 133.2 %copy-start.7 = (f32[1,3072]{1,0:T(1,128)S(1)}, f32[1,3072]{1,0:T(1,128)}, u32[]{:S(2)}) copy-start(f32[1,3072]{1,0:T(1,128)} %param.15) | copy-start | bytes 36868
  45.5 2.1 collective-permute-start.1
  59.1 382.0 %all-reduce.14.cloned.1.call-start = ((), (), s32[]{:S(2)}) async-start(), calls=%async_computation.1 | async-start | bytes 393216
  60.5 253.7 %collective-permute-start.2 = (f32[1,384]{1,0:T(1,128)S(1)}, f32[1,384]{1,0:T(1,128)S(1)}, u32[]{:S(2)}, u32[]{:S(2)}) collective-permute-start(f32[1,384]{1,0:T(1,128)S(1)} %slice.71), channel_id=1, source_target_pairs={{16,0},{32,16},{48,32},{64,48},{80,64},{96,80},{112,96},{128,112},... | collective-permute-start | bytes 4616 | tf_op jit(solution)/shard_map/ppermute | solution.py:15
  314.8 2.5 collective-permute-start.3
  328.9 375.8 %all-reduce.16.cloned.1.call-start = ((), (), s32[]{:S(2)}) async-start(), calls=%async_computation.2 | async-start | bytes 393216
  329.0 248.8 %collective-permute-start.4 = (f32[1,384]{1,0:T(1,128)S(1)}, f32[1,384]{1,0:T(1,128)S(1)}, u32[]{:S(2)}, u32[]{:S(2)}) collective-permute-start(f32[1,384]{1,0:T(1,128)S(1)} %slice.75), channel_id=1, source_target_pairs={{16,0},{32,16},{48,32},{64,48},{80,64},{96,80},{112,96},{128,112},... | collective-permute-start | bytes 4616 | tf_op jit(solution)/shard_map/ppermute | solution.py:15
  578.4 2.5 collective-permute-start.5
  592.5 375.6 %all-reduce.18.cloned.1.call-start = ((), (), s32[]{:S(2)}) async-start(), calls=%async_computation.3 | async-start | bytes 393216
  592.5 248.6 %collective-permute-start.6 = (f32[1,384]{1,0:T(1,128)S(1)}, f32[1,384]{1,0:T(1,128)S(1)}, u32[]{:S(2)}, u32[]{:S(2)}) collective-permute-start(f32[1,384]{1,0:T(1,128)S(1)} %slice.79), channel_id=1, source_target_pairs={{16,0},{32,16},{48,32},{64,48},{80,64},{96,80},{112,96},{128,112},... | collective-permute-start | bytes 4616 | tf_op jit(solution)/shard_map/ppermute | solution.py:15
  841.8 2.5 collective-permute-start.7
Sparse Core Ops, SparseCore 0:
  59.2 118.2 all-reduce.11
  329.0 112.0 all-reduce.13
  592.6 112.0 all-reduce.15
  855.9 112.0 all-reduce.17
where the time goes:
time: 978 us; the launch traced here: 977 us
  waiting for transfers between devices  452 us (46%)
  blocking collectives  402 us (41%)
  matrix products  67.2 us (7%)
  between operations  22.5 us (2%)
  other arithmetic  15.1 us (2%)
  starting transfers between devices  12 us (1%)
    unnamed x8, waiting for transfers between devices  450 us
    psum x3, blocking collectives, shards(): dual_sq = lax.psum(dual_local, ('tm', 'bat'))  309 us
    all_gather x4, blocking collectives, couple_backward(): lax.all_gather(duals, 'bat', axis=0, tiled=True)  92.9 us
    dot_general x4, matrix products, feeder_apply(): jnp.einsum('rjk,jmk->rjm', picked, block_values, precision=HIGH)  36.7 us
    dot_general x4, matrix products, feeder_adjoint(): pushed = jnp.einsum('rjm,jmk->rjk', chosen, block_values, precision=HIGH)  23.3 us
  transfers between devices with their start and end apart: 12, of which 8 were waited for; matrix products, arithmetic and copies ran while one was open for 4% of the time, Pallas kernels for 0%

commit v1 on v0

--- a/solution.py
+++ b/solution.py
@@ -2,6 +2,7 @@
 import jax.numpy as jnp
 from jax import lax
 from jax.sharding import PartitionSpec as P
+from jax.lax import all_to_all, axis_size
 
 ITERS = 4
 HIGH = lax.Precision.HIGHEST
@@ -70,7 +71,10 @@
 
     def couple_backward(duals):
         return feeder_adjoint(
-            lax.all_gather(duals, "bat", axis=0, tiled=True), block_values, rows_tab, local_tab
+            jnp.concatenate(all_to_all(jnp.stack([duals] * axis_size("bat")), "bat", 0, 0), axis=0),
+            block_values,
+            rows_tab,
+            local_tab,
         )
 
     power, charge, dyn_dual, feeder_dual = (power0, charge0, dyn_dual0, feeder_dual0)

time: 978 us -> 930 us (0.951)
  blocking collectives: 402 us -> 313 us
  starting transfers between devices: 12 us -> 39 us
    all_gather x4 -> x0, blocking collectives: 92.9 us -> none  [couple_backward(): lax.all_gather(duals, 'bat', axis=0, tiled=True)]
    all_to_all x0 -> x4, starting transfers between devices: none -> 27.2 us  [couple_backward(): all_to_all(jnp.stack([duals] * axis_size('bat')), 'bat', 0, 0)]
  transfers between devices with their start and end apart: 12 -> 16, of which waited for: 8 -> 9; matrix products, arithmetic and copies ran while one was open for 4% -> 4% of each run, Pallas kernels for 0% -> 0%
where the time goes in v1:
time: 930 us; the launch traced here: 928 us
  waiting for transfers between devices  460 us (49%)
  blocking collectives  313 us (34%)
  matrix products  67.2 us (7%)
  starting transfers between devices  39 us (4%)
  between operations  22.5 us (2%)
  other arithmetic  15.8 us (2%)
  local copies, waits for them, and re-layouts  10.3 us (1%)
    unnamed x8, waiting for transfers between devices  452 us
    psum x3, blocking collectives, shards(): dual_sq = lax.psum(dual_local, ('tm', 'bat'))  313 us
    dot_general x4, matrix products, feeder_apply(): jnp.einsum('rjk,jmk->rjm', picked, block_values, precision=HIGH)  36.7 us
    all_to_all x4, starting transfers between devices, couple_backward(): all_to_all(jnp.stack([duals] * axis_size('bat')), 'bat', 0, 0)  27.2 us
    dot_general x4, matrix products, feeder_adjoint(): pushed = jnp.einsum('rjm,jmk->rjk', chosen, block_values, precision=HIGH)  23.3 us
  transfers between devices with their start and end apart: 16, of which 9 were waited for; matrix products, arithmetic and copies ran while one was open for 4% of the time, Pallas kernels for 0%

profile of v1, /device:TPU:2, one launch (start us, length us, event | category | flops | bytes accessed | tf_op | source)
XLA Modules:
  0.0 928.1 jit_solution(6738354166904598073)
XLA Ops:
  8.8 9.2 all-to-all-start
  25.5 5.8 convolution_bitcast_fusion.15
  36.0 9.2 convolution_bitcast_fusion.14
  47.7 118.1 %all-reduce.12.cloned.1.call-done = f32[16,3072]{1,0:T(8,128)} async-done(((f32[16,3072]{1,0:T(8,128)}), f32[16,3072]{1,0:T(8,128)}) %all-reduce.12.cloned.1.call-update) | async-done | bytes 196624
  165.8 2.2 multiply_reduce_fusion.5
  168.7 5.8 all-to-all-start.1
  177.1 105.4 %all-reduce.6 = (f32[]{:T(128)}, f32[]{:T(128)}) all-reduce(f32[]{:T(128)S(6)} %add.99, f32[]{:T(128)} %get-tuple-element.31), channel_id=1, replica_groups=mesh['tm'=32,'bat'=16] {'tm','bat'}, use_global_device_ids=true, to_apply=%region_4.5 | all-reduce | flops 2 | bytes 16 | tf_op jit(solution)/shard_map/psum | solution.py:115
  284.4 5.8 convolution_bitcast_fusion.13
  295.0 9.2 convolution_bitcast_fusion.12
  305.4 113.0 %all-reduce.14.cloned.1.call-done = f32[16,3072]{1,0:T(8,128)} async-done(((f32[16,3072]{1,0:T(8,128)}), f32[16,3072]{1,0:T(8,128)}) %all-reduce.14.cloned.1.call-update) | async-done | bytes 196624
  418.3 2.2 multiply_reduce_fusion.4
  421.3 5.8 all-to-all-start.2
  429.7 105.4 %all-reduce.5 = (f32[]{:T(128)}, f32[]{:T(128)}) all-reduce(f32[]{:T(128)S(6)} %add.106, f32[]{:T(128)} %get-tuple-element.23), channel_id=1, replica_groups=mesh['tm'=32,'bat'=16] {'tm','bat'}, use_global_device_ids=true, to_apply=%region_10.11 | all-reduce | flops 2 | bytes 16 | tf_op jit(solution)/shard_map/psum | solution.py:115
  537.0 5.8 convolution_bitcast_fusion.11
  547.5 9.2 convolution_bitcast_fusion.10
  559.3 111.6 %all-reduce.16.cloned.1.call-done = f32[16,3072]{1,0:T(8,128)} async-done(((f32[16,3072]{1,0:T(8,128)}), f32[16,3072]{1,0:T(8,128)}) %all-reduce.16.cloned.1.call-update) | async-done | bytes 196624
  670.9 2.2 multiply_reduce_fusion.3
  674.4 102.2 %all-reduce.4 = (f32[]{:T(128)}, f32[]{:T(128)}) all-reduce(f32[]{:T(128)S(6)} %add.113, f32[]{:T(128)} %get-tuple-element.15), channel_id=1, replica_groups=mesh['tm'=32,'bat'=16] {'tm','bat'}, use_global_device_ids=true, to_apply=%region_16.17 | all-reduce | flops 2 | bytes 16 | tf_op jit(solution)/shard_map/psum | solution.py:115
  778.8 6.5 all-to-all-start.3
  787.2 5.1 all-to-all-done.3
  792.8 5.8 convolution_bitcast_fusion.9
  800.2 9.2 convolution_bitcast_fusion.8
  810.6 108.8 %all-reduce.18.cloned.1.call-done = f32[16,3072]{1,0:T(8,128)} async-done(((f32[16,3072]{1,0:T(8,128)}), f32[16,3072]{1,0:T(8,128)}) %all-reduce.18.cloned.1.call-update) | async-done | bytes 196624
  919.4 2.1 fusion.92
  (103 shorter events, 40.2 us)
Async XLA Ops:
  7.2 24.6 %copy-start.2 = (f32[16,384]{1,0:T(8,128)S(1)}, f32[16,384]{1,0:T(8,128)}, u32[]{:S(2)}) copy-start(f32[16,384]{1,0:T(8,128)} %param.14) | copy-start | bytes 73732
  7.2 24.6 %copy-start.6 = (f32[384]{0:T(512)S(1)}, f32[384]{0:T(512)}, u32[]{:S(2)}) copy-start(f32[384]{0:T(512)} %param.18) | copy-start | bytes 4612
  7.2 24.6 %copy-start.4 = (f32[16,384]{1,0:T(8,128)S(1)}, f32[16,384]{1,0:T(8,128)}, u32[]{:S(2)}) copy-start(f32[16,384]{1,0:T(8,128)} %param.12) | copy-start | bytes 73732
  7.2 24.6 %copy-start.5 = (f32[16,384]{1,0:T(8,128)S(1)}, f32[16,384]{1,0:T(8,128)}, u32[]{:S(2)}) copy-start(f32[16,384]{1,0:T(8,128)} %param.13) | copy-start | bytes 73732
  7.2 24.6 %copy-start.1 = (f32[16,384]{1,0:T(8,128)S(1)}, f32[16,384]{1,0:T(8,128)}, u32[]{:S(2)}) copy-start(f32[16,384]{1,0:T(8,128)} %param.16) | copy-start | bytes 73732
  7.2 27.7 %copy-start = (f32[16,384]{1,0:T(8,128)S(1)}, f32[16,384]{1,0:T(8,128)}, u32[]{:S(2)}) copy-start(f32[16,384]{1,0:T(8,128)} %param.17) | copy-start | bytes 73732
  8.8 16.3 %all-to-all-start = ((f32[16,1,3072]{2,1,0:T(1,128)}), f32[16,1,3072]{2,1,0:T(1,128)S(1)}, u32[]{:S(2)}, u32[]{:S(2)}) async-start(f32[16,1,3072]{2,1,0:T(1,128)} %stack.8), calls=%async_computation | async-start | bytes 393216 | tf_op jit(solution)/shard_map/all_to_all | solution.py:74
  18.0 147.8 %all-reduce.12.cloned.1.call-start = ((), (), s32[]{:S(2)}) async-start(), calls=%async_computation.4 | async-start | bytes 393216
  18.7 13.1 %collective-permute-start = (f32[1,384]{1,0:T(1,128)S(1)}, f32[1,384]{1,0:T(1,128)S(1)}, u32[]{:S(2)}, u32[]{:S(2)}) collective-permute-start(f32[1,384]{1,0:T(1,128)S(1)} %slice.53), channel_id=1, source_target_pairs={{16,0},{32,16},{48,32},{64,48},{80,64},{96,80},{112,96},{128,112},... | collective-permute-start | bytes 4616 | tf_op jit(solution)/shard_map/ppermute | solution.py:16
  31.3 134.4 %copy-start.3 = (f32[3072]{0:T(1024)S(1)}, f32[3072]{0:T(1024)}, u32[]{:S(2)}) copy-start(f32[3072]{0:T(1024)} %param.20) | copy-start | bytes 36868
  31.3 134.4 %copy-start.7 = (f32[1,3072]{1,0:T(1,128)S(1)}, f32[1,3072]{1,0:T(1,128)}, u32[]{:S(2)}) copy-start(f32[1,3072]{1,0:T(1,128)} %param.15) | copy-start | bytes 36868
  32.5 2.4 collective-permute-start.1
  168.7 115.3 %all-to-all-start.1 = ((f32[16,1,3072]{2,1,0:T(1,128)}), f32[16,1,3072]{2,1,0:T(1,128)S(1)}, u32[]{:S(2)}, u32[]{:S(2)}) async-start(f32[16,1,3072]{2,1,0:T(1,128)} %stack.9), calls=%async_computation.1 | async-start | bytes 393216 | tf_op jit(solution)/shard_map/all_to_all | solution.py:74
  174.5 243.9 %all-reduce.14.cloned.1.call-start = ((), (), s32[]{:S(2)}) async-start(), calls=%async_computation.5 | async-start | bytes 393216
  174.5 116.2 %collective-permute-start.2 = (f32[1,384]{1,0:T(1,128)S(1)}, f32[1,384]{1,0:T(1,128)S(1)}, u32[]{:S(2)}, u32[]{:S(2)}) collective-permute-start(f32[1,384]{1,0:T(1,128)S(1)} %slice.71), channel_id=1, source_target_pairs={{16,0},{32,16},{48,32},{64,48},{80,64},{96,80},{112,96},{128,112},... | collective-permute-start | bytes 4616 | tf_op jit(solution)/shard_map/ppermute | solution.py:16
  291.3 2.5 collective-permute-start.3
  421.3 115.3 %all-to-all-start.2 = ((f32[16,1,3072]{2,1,0:T(1,128)}), f32[16,1,3072]{2,1,0:T(1,128)S(1)}, u32[]{:S(2)}, u32[]{:S(2)}) async-start(f32[16,1,3072]{2,1,0:T(1,128)} %stack.10), calls=%async_computation.2 | async-start | bytes 393216 | tf_op jit(solution)/shard_map/all_to_all | solution.py:74
  427.0 243.9 %all-reduce.16.cloned.1.call-start = ((), (), s32[]{:S(2)}) async-start(), calls=%async_computation.6 | async-start | bytes 393216
  427.1 116.2 %collective-permute-start.4 = (f32[1,384]{1,0:T(1,128)S(1)}, f32[1,384]{1,0:T(1,128)S(1)}, u32[]{:S(2)}, u32[]{:S(2)}) collective-permute-start(f32[1,384]{1,0:T(1,128)S(1)} %slice.75), channel_id=1, source_target_pairs={{16,0},{32,16},{48,32},{64,48},{80,64},{96,80},{112,96},{128,112},... | collective-permute-start | bytes 4616 | tf_op jit(solution)/shard_map/ppermute | solution.py:16
  543.9 2.5 collective-permute-start.5
  558.0 227.4 %collective-permute-start.6 = (f32[1,384]{1,0:T(1,128)S(1)}, f32[1,384]{1,0:T(1,128)S(1)}, u32[]{:S(2)}, u32[]{:S(2)}) collective-permute-start(f32[1,384]{1,0:T(1,128)S(1)} %slice.79), channel_id=1, source_target_pairs={{16,0},{32,16},{48,32},{64,48},{80,64},{96,80},{112,96},{128,112},... | collective-permute-start | bytes 4616 | tf_op jit(solution)/shard_map/ppermute | solution.py:16
  778.8 13.5 %all-to-all-start.3 = ((f32[16,1,3072]{2,1,0:T(1,128)}), f32[16,1,3072]{2,1,0:T(1,128)S(1)}, u32[]{:S(2)}, u32[]{:S(2)}) async-start(f32[16,1,3072]{2,1,0:T(1,128)} %stack.11), calls=%async_computation.3 | async-start | bytes 393216 | tf_op jit(solution)/shard_map/all_to_all | solution.py:74
  785.3 134.1 %all-reduce.18.cloned.1.call-start = ((), (), s32[]{:S(2)}) async-start(), calls=%async_computation.7 | async-start | bytes 393216
  786.0 13.1 %collective-permute-start.7 = (f32[1,384]{1,0:T(1,128)S(1)}, f32[1,384]{1,0:T(1,128)S(1)}, u32[]{:S(2)}, u32[]{:S(2)}) collective-permute-start(f32[1,384]{1,0:T(1,128)S(1)} %slice.80), channel_id=1, source_target_pairs={{0,16},{16,32},{32,48},{48,64},{64,80},{80,96},{96,112},{112,128},... | collective-permute-start | bytes 4616 | tf_op jit(solution)/shard_map/ppermute | solution.py:16
  (1 other events, 24.6 us)
Sparse Core Ops, SparseCore 0:
  46.5 119.2 all-reduce.11
  305.5 112.8 all-reduce.13
  558.1 112.8 all-reduce.15
  810.7 108.6 all-reduce.17
